TPU v7x, 128 devices: a whole 4x4x4 slice. The times are simulated.
128 devices in a mesh: dp: 16 (over z, y), tensor: 8 (over x, core).
Axes of the slice: x: 4, y: 4, z: 4, core: 2. Of those that a mesh axis runs over, the one named last changes fastest.
Arguments:
- dense: bfloat16 [3072, 2048], P('dp'), may hold values from -8 to 8
- bottom_weight: bfloat16 [2048, 16384], P(None, 'tensor'), may hold values from -0.125 to 0.125
- bottom_bias: float32 [16384], P('tensor'), may hold values from -3 to 3
- cross_blocks: bfloat16 [80, 512, 512], P('tensor', 'dp'), may hold values from -0.25 to 0.25
- cross_bias: float32 [16384], P('tensor'), may hold values from -3 to 3
- cotangent: bfloat16 [3072, 16384], P('dp', 'tensor'), may hold values from -6 to 6
- in_blocks: int32 [8, 10], replicated, may hold values from 0 to 31, as said below
- out_blocks: int32 [8, 10], replicated, may hold values from 0 to 31, as said below
- live_slots: int32 [8], replicated, may hold values from 2 to 10, as said below
Outputs:
- cross_out: bfloat16 [3072, 16384], P('dp', 'tensor')
- grad_bottom: float32 [2048, 16384], P('dp', 'tensor')
- grad_bias_bottom: float32 [16384], P('tensor')
- grad_blocks: float32 [80, 512, 512], P('tensor', 'dp')
- grad_bias: float32 [16384], P('tensor')
Inputs may be any that keep to these rules, and one draw needn't show every extreme that they name: `in_blocks`: among the live slots of one tensor device, at most 2 have input blocks held by any one tensor device (blocks s * 16384 / (512 * 8) onward for device s), and this most is reached in every draw. `out_blocks`: among the live slots of one tensor device, at most 2 have output blocks held by any one tensor device, and this most is reached in every draw. `live_slots`: some tensor device has all 10 slots live.
All inputs are finite; a program needn't handle non-finite values.
Results may differ from a plain program's by a relative error of at most 0.014.
Values may be sent and summed in bfloat16 or wider, within the bound.
A program may use at most 128 MiB of HBM per device.

v0:
```python
import jax
import jax.numpy as jnp
from jax import lax
from jax.sharding import PartitionSpec as P

BLK = 512
SLOTS = 10


def slot_ranks(owner, alive):
    order = jnp.arange(owner.shape[1])
    earlier = order[None, :] < order[:, None]
    same = (owner[:, :, None] == owner[:, None, :]) & alive[:, None, :] & earlier[None, :, :]
    return jnp.sum(same.astype(jnp.int32), axis=2)


def post_table(owner_mine, rank_mine, alive_mine, groups, capacity):
    slot_count = owner_mine.shape[0]
    match = (
        (owner_mine[None, None, :] == jnp.arange(groups)[:, None, None])
        & (rank_mine[None, None, :] == jnp.arange(capacity)[None, :, None])
        & alive_mine[None, None, :]
    )
    chosen = jnp.sum(match.astype(jnp.int32) * jnp.arange(slot_count)[None, None, :], axis=2)
    filled = jnp.any(match, axis=2)
    return (chosen, filled)


def pack_parts(parts, chosen, filled):
    picked = jnp.take(parts, chosen.reshape(-1), axis=1) * filled.reshape(-1)[None, :, None].astype(
        parts.dtype
    )
    return picked.reshape(parts.shape[0], chosen.shape[0], chosen.shape[1] * parts.shape[2])


def collect_parts(received, owner, local, rank, alive, target, capacity, per_device):
    row_count, groups, span_width = received.shape
    block_width = span_width // capacity
    match = ((owner == target) & alive)[:, :, None] & (
        rank[:, :, None] == jnp.arange(capacity)[None, None, :]
    )
    matches = match[:, :, :, None] & (
        local[:, :, None, None] == jnp.arange(per_device)[None, None, None, :]
    )
    onehot = (
        jnp.sum(matches.astype(jnp.int32), axis=1)
        .reshape(groups * capacity, per_device)
        .astype(jnp.bfloat16)
    )
    flattened = received.reshape(row_count, groups * capacity, block_width)
    summed = jnp.einsum("rib,il->rlb", flattened, onehot, preferred_element_type=jnp.float32)
    return summed.reshape(row_count, per_device * block_width)


def on_device(
    dense,
    bottom_weight,
    bottom_bias,
    cross_blocks,
    cross_bias,
    cotangent,
    in_blocks,
    out_blocks,
    live_slots,
):
    groups = lax.axis_size("tensor")
    mine = lax.axis_index("tensor")
    row_count = dense.shape[0]
    local_width = bottom_weight.shape[1]
    per_device = local_width // BLK
    capacity = -(-SLOTS // groups)
    preact = jnp.dot(dense, bottom_weight, preferred_element_type=jnp.float32) + bottom_bias
    start = jax.nn.silu(preact).astype(jnp.bfloat16)
    start_wide = start.astype(jnp.float32)
    cot_wide = cotangent.astype(jnp.float32)
    grad_mixed = cot_wide * start_wide
    grad_mixed_low = grad_mixed.astype(jnp.bfloat16)
    alive = jnp.arange(SLOTS)[None, :] < live_slots[:, None]
    alive_mine = alive[mine]
    switch = alive_mine.astype(jnp.bfloat16)[None, :, None]
    in_owner = in_blocks // per_device
    in_local = in_blocks % per_device
    out_owner = out_blocks // per_device
    out_local = out_blocks % per_device
    in_rank = slot_ranks(in_owner, alive)
    out_rank = slot_ranks(out_owner, alive)
    whole_start = lax.all_gather(start, "tensor", axis=1, tiled=True)
    fetched = jnp.take(whole_start.reshape(row_count, -1, BLK), in_blocks[mine], axis=1)
    taken = fetched
    product = jnp.einsum(
        "rki,kij->rkj",
        taken,
        lax.all_gather(cross_blocks, "dp", axis=1, tiled=True),
        preferred_element_type=jnp.float32,
    )
    parts = product.astype(jnp.bfloat16) * switch
    chosen_out, filled_out = post_table(
        out_owner[mine], out_rank[mine], alive_mine, groups, capacity
    )
    arrived_parts = lax.all_to_all(
        pack_parts(parts, chosen_out, filled_out), "tensor", split_axis=1, concat_axis=1, tiled=True
    )
    mixed = (
        collect_parts(
            arrived_parts, out_owner, out_local, out_rank, alive, mine, capacity, per_device
        )
        + cross_bias
    )
    cross_out = (start_wide * mixed + start_wide).astype(jnp.bfloat16)
    whole_grad = lax.all_gather(grad_mixed_low, "tensor", axis=1, tiled=True)
    upstream = jnp.take(whole_grad.reshape(row_count, -1, BLK), out_blocks[mine], axis=1)
    upstream = upstream * switch
    backward = jnp.einsum(
        "rkj,kij->rki",
        upstream,
        lax.all_gather(cross_blocks, "dp", axis=1, tiled=True),
        preferred_element_type=jnp.float32,
    )
    back_parts = backward.astype(jnp.bfloat16)
    chosen_in, filled_in = post_table(in_owner[mine], in_rank[mine], alive_mine, groups, capacity)
    arrived_back = lax.all_to_all(
        pack_parts(back_parts, chosen_in, filled_in),
        "tensor",
        split_axis=1,
        concat_axis=1,
        tiled=True,
    )
    grad_start = collect_parts(
        arrived_back, in_owner, in_local, in_rank, alive, mine, capacity, per_device
    )
    block_terms = jnp.einsum("rki,rkj->kij", fetched, upstream, preferred_element_type=jnp.float32)
    grad_blocks = lax.psum_scatter(
        block_terms.astype(jnp.bfloat16), "dp", scatter_dimension=1, tiled=True
    ).astype(jnp.float32)
    grad_start = grad_start + cot_wide * mixed + cot_wide
    sigma = jax.nn.sigmoid(preact)
    grad_pre = grad_start * sigma * (1.0 + preact * (1.0 - sigma))
    grad_pre_low = grad_pre.astype(jnp.bfloat16)
    taken = dense
    grad_bottom = lax.psum_scatter(
        lax.dot_general(
            taken, grad_pre_low, (((0,), (0,)), ((), ())), preferred_element_type=jnp.float32
        ).astype(jnp.bfloat16),
        "dp",
        scatter_dimension=0,
        tiled=True,
    ).astype(jnp.float32)
    bias_sums = lax.psum((jnp.sum(grad_pre, axis=0), jnp.sum(grad_mixed, axis=0)), "dp")
    return (cross_out, grad_bottom, bias_sums[0], grad_blocks, bias_sums[1])


def solution(mesh):
    return jax.shard_map(
        on_device,
        mesh=mesh,
        in_specs=(
            P("dp", None),
            P(None, "tensor"),
            P("tensor"),
            P("tensor", "dp", None),
            P("tensor"),
            P("dp", "tensor"),
            P(),
            P(),
            P(),
        ),
        out_specs=(
            P("dp", "tensor"),
            P("dp", "tensor"),
            P("tensor"),
            P("tensor", "dp", None),
            P("tensor"),
        ),
        check_vma=False,
    )
```

profile of v0, /device:TPU:0, one launch (start us, length us, event | category | flops | bytes accessed | tf_op | source)
XLA Modules:
  0.0 400.9 jit_solution(8510571627176802936)
XLA Ops:
  8.3 7.8 %fusion.9 = (f32[2048]{0:T(1024)}, bf16[192,2048]{1,0:T(8,128)(2,1)}, f32[192,2048]{1,0:T(8,128)}) fusion(bf16[192,2048]{1,0:T(8,128)(2,1)} %param.18, f32[2048]{0:T(1024)} %param.15, bf16[192,2048]{1,0:T(8,128)(2,1)S(1)} %copy-done, bf16[2048,2048]{1,0:T(8,128)(2,1)} %param.14), kind=kOutput, calls=%fused_computation.28 | convolution fusion | flops 1614542848 | bytes 12337152 | tf_op jit(solution)/shard_map/dot_general | solution.py:72
  16.2 2.3 fusion.10
  21.2 38.5 %all-gather.4.cloned.1.call-done = bf16[192,16384]{1,0:T(8,128)(2,1)} async-done(((bf16[192,2048]{1,0:T(8,128)(2,1)}), bf16[192,16384]{1,0:T(8,128)(2,1)}) %all-gather.4.cloned.1.call-update) | async-done | bytes 6291472 | tf_op jit(solution)/shard_map/all_gather | solution.py:87
  59.6 6.2 %copy.90 = bf16[24,32,8,512]{3,2,0,1:T(8,128)(2,1)} copy(bf16[24,32,8,512]{3,2,1,0:T(8,128)(2,1)} %bitcast.71) | data formatting | bytes 12582912 | tf_op jit(solution)/shard_map/reshape | solution.py:88
  65.8 37.0 %all-gather.8.cloned.1.call-done = bf16[192,16384]{1,0:T(8,128)(2,1)} async-done(((bf16[192,2048]{1,0:T(8,128)(2,1)}), bf16[192,16384]{1,0:T(8,128)(2,1)}) %all-gather.8.cloned.1.call-update) | async-done | bytes 6291472 | tf_op jit(solution)/shard_map/all_gather | solution.py:110
  102.9 6.3 %copy.89 = bf16[24,32,8,512]{3,2,0,1:T(8,128)(2,1)} copy(bf16[24,32,8,512]{3,2,1,0:T(8,128)(2,1)} %bitcast.72) | data formatting | bytes 12582912 | tf_op jit(solution)/shard_map/reshape | solution.py:111
  109.2 4.9 %gather_fusion = bf16[10,192,512]{2,1,0:T(8,128)(2,1)} fusion(bf16[192,32,512]{2,0,1:T(8,128)(2,1)} %bitcast.69, s32[1024]{0:T(1024)S(1)} %pad_clamp_fusion.3), kind=kCustom, calls=%fused_computation.clone | custom fusion | bytes 3932200 | tf_op jit(solution)/shard_map/jit(_take)/gather | solution.py:88
  114.0 3.7 gather_fusion.2
  117.8 5.8 %convolution_convert_fusion = bf16[10,512,512]{2,1,0:T(8,128)(2,1)} fusion(bf16[10,192,512]{2,1,0:T(8,128)(2,1)} %gather_fusion, pred[10]{0:T(512)(128)(4,1)} %get-tuple-element.65, bf16[10,192,512]{2,1,0:T(8,128)(2,1)S(1)} %gather_fusion.2, pred[10]{0:T(512)(128)(4,1)S(1)} %get-tuple-element.44, bf16[10]{0:T(256)(128)(2,1)} %get-tuple-element.50), kind=kOutput, calls=%fused_computation.9 | convolution fusion | flops 1012203520 | bytes 9175080 | tf_op jit(solution)/shard_map/rki,rkj->kij/dot_general | solution.py:131
  127.7 1.4 fusion.14
  129.7 1.3 copy.61
  131.0 1.4 reshape.262
  132.4 1.5 select_reduce_fusion
  133.8 1.3 copy.59
  138.9 22.7 %all-gather.6.cloned.1.call-done = bf16[10,512,512]{2,1,0:T(8,128)(2,1)} async-done(((bf16[10,32,512]{2,1,0:T(8,128)(2,1)}), bf16[10,512,512]{2,1,0:T(8,128)(2,1)}) %all-gather.6.cloned.1.call-update) | async-done | bytes 5242896 | tf_op jit(solution)/shard_map/all_gather | solution.py:93
  161.6 5.7 %multiply_bitcast_fusion = bf16[192,10,512]{2,0,1:T(8,128)(2,1)} fusion(bf16[10,512,512]{2,1,0:T(8,128)(2,1)} %all-gather.6.cloned.1.call-done, bf16[10]{0:T(256)(128)(2,1)} %get-tuple-element.50, bf16[10,192,512]{2,1,0:T(8,128)(2,1)} %gather_fusion, pred[10]{0:T(512)(128)(4,1)} %get-tuple-element.65), kind=kOutput, calls=%fused_computation.20 | convolution fusion | flops 1009582080 | bytes 9175070 | tf_op jit(solution)/shard_map/rki,kij->rkj/dot_general | solution.py:90
  167.3 4.0 %gather_fusion.1 = bf16[16,192,512]{2,1,0:T(8,128)(2,1)} fusion(bf16[192,10,512]{2,0,1:T(8,128)(2,1)} %multiply_bitcast_fusion, s32[1024]{0:T(1024)} %pad_clamp_fusion.2), kind=kCustom, calls=%fused_computation.1.clone | custom fusion | bytes 6291520 | tf_op jit(solution)/shard_map/jit(_take)/gather | solution.py:30
  171.4 2.3 bitcast_multiply_fusion.1
  173.6 3.4 copy.62
  177.1 5.7 %reshape.254 = bf16[192,8,1024]{2,1,0:T(8,128)(2,1)} reshape(bf16[192,16,512]{2,1,0:T(8,128)(2,1)} %copy.62) | data formatting | bytes 6291456 | tf_op jit(solution)/shard_map/reshape | solution.py:33
  182.8 5.4 %copy.63 = bf16[192,8,1024]{2,0,1:T(8,128)(2,1)} copy(bf16[192,8,1024]{2,1,0:T(8,128)(2,1)} %reshape.254) | data formatting | bytes 6291456 | tf_op jit(solution)/shard_map/reshape | solution.py:33
  188.1 4.6 %all-to-all-start = ((bf16[192,8,1024]{2,0,1:T(8,128)(2,1)}), bf16[192,8,1024]{2,0,1:T(8,128)(2,1)}, u32[]{:S(2)}, u32[]{:S(2)}) async-start(bf16[192,8,1024]{2,0,1:T(8,128)(2,1)} %copy.63), calls=%async_computation | async-start | bytes 6291456 | tf_op jit(solution)/shard_map/all_to_all | solution.py:100
  193.9 1.3 copy.71
  195.2 1.4 reshape.263
  196.6 1.3 copy.69
  197.9 1.3 reshape.258
  201.6 5.8 %convert_bitcast_fusion.1 = bf16[192,10,512]{2,0,1:T(8,128)(2,1)} fusion(bf16[10,512,512]{2,1,0:T(8,128)(2,1)} %all-gather.6.cloned.1.call-done, bf16[10,192,512]{2,1,0:T(8,128)(2,1)S(1)} %gather_fusion.2, pred[10]{0:T(512)(128)(4,1)} %copy-done.21, bf16[10]{0:T(256)(128)(2,1)} %get-tuple-element.50), kind=kOutput, calls=%fused_computation.19 | convolution fusion | flops 1009582080 | bytes 9175070 | tf_op jit(solution)/shard_map/rkj,kij->rki/dot_general | solution.py:113
  207.4 4.1 %gather_fusion.3 = bf16[16,192,512]{2,1,0:T(8,128)(2,1)} fusion(bf16[192,10,512]{2,0,1:T(8,128)(2,1)} %convert_bitcast_fusion.1, s32[1024]{0:T(1024)} %pad_clamp_fusion), kind=kCustom, calls=%fused_computation.3.clone | custom fusion | bytes 6291520 | tf_op jit(solution)/shard_map/jit(_take)/gather | solution.py:30
  211.6 2.3 bitcast_multiply_fusion
  213.8 3.5 copy.72
  217.3 5.7 %reshape.259 = bf16[192,8,1024]{2,1,0:T(8,128)(2,1)} reshape(bf16[192,16,512]{2,1,0:T(8,128)(2,1)} %copy.72) | data formatting | bytes 6291456 | tf_op jit(solution)/shard_map/reshape | solution.py:33
  223.0 5.3 %copy.73 = bf16[192,8,1024]{2,0,1:T(8,128)(2,1)} copy(bf16[192,8,1024]{2,1,0:T(8,128)(2,1)} %reshape.259) | data formatting | bytes 6291456 | tf_op jit(solution)/shard_map/reshape | solution.py:33
  228.3 2.9 all-to-all-done
  231.2 4.4 %all-to-all-start.1 = ((bf16[192,8,1024]{2,0,1:T(8,128)(2,1)}), bf16[192,8,1024]{2,0,1:T(8,128)(2,1)}, u32[]{:S(2)}, u32[]{:S(2)}) async-start(bf16[192,8,1024]{2,0,1:T(8,128)(2,1)} %copy.73), calls=%async_computation.1 | async-start | bytes 6291456 | tf_op jit(solution)/shard_map/all_to_all | solution.py:121
  236.6 5.3 %copy.64 = bf16[192,8,1024]{2,1,0:T(8,128)(2,1)} copy(bf16[192,8,1024]{2,0,1:T(8,128)(2,1)} %all-to-all-done) | data formatting | bytes 6291456 | tf_op jit(solution)/shard_map/all_to_all | solution.py:100
  241.9 5.7 %reshape.255 = bf16[192,16,512]{2,1,0:T(8,128)(2,1)} reshape(bf16[192,8,1024]{2,1,0:T(8,128)(2,1)} %copy.64) | data formatting | bytes 6291456 | tf_op jit(solution)/shard_map/reshape | solution.py:50
  247.6 2.5 fusion.29
  250.7 23.4 %all-to-all-done.1 = bf16[192,8,1024]{2,0,1:T(8,128)(2,1)} async-done(((bf16[192,8,1024]{2,0,1:T(8,128)(2,1)}), bf16[192,8,1024]{2,0,1:T(8,128)(2,1)}, u32[]{:S(2)}, u32[]{:S(2)}) %all-to-all-start.1) | async-done | bytes 3145760 | tf_op jit(solution)/shard_map/all_to_all | solution.py:121
  274.0 5.2 %copy.74 = bf16[192,8,1024]{2,1,0:T(8,128)(2,1)} copy(bf16[192,8,1024]{2,0,1:T(8,128)(2,1)} %all-to-all-done.1) | data formatting | bytes 6291456 | tf_op jit(solution)/shard_map/all_to_all | solution.py:121
  279.3 5.6 %reshape.260 = bf16[192,16,512]{2,1,0:T(8,128)(2,1)} reshape(bf16[192,8,1024]{2,1,0:T(8,128)(2,1)} %copy.74) | data formatting | bytes 6291456 | tf_op jit(solution)/shard_map/reshape | solution.py:50
  284.9 2.5 fusion.30
  289.1 1.9 fusion.26
  290.9 5.6 %convert_bitcast_fusion = bf16[2048,2048]{0,1:T(8,128)(2,1)} fusion(bf16[192,2048]{1,0:T(8,128)(2,1)S(1)} %copy-done, bf16[192,2048]{1,0:T(8,128)(2,1)S(1)} %get-tuple-element.43), kind=kOutput, calls=%fused_computation.4 | convolution fusion | flops 1614807040 | bytes 9961472 | tf_op jit(solution)/shard_map/dot_general | solution.py:141
  296.6 12.3 %copy.81 = bf16[2048,2048]{1,0:T(8,128)(2,1)} copy(bf16[2048,2048]{0,1:T(8,128)(2,1)} %convert_bitcast_fusion) | data formatting | bytes 16777216
  309.5 72.9 %all-reduce = (f32[2048]{0:T(1024)}, f32[2048]{0:T(1024)}) all-reduce(f32[2048]{0:T(1024)S(1)} %get-tuple-element.42, f32[2048]{0:T(1024)S(1)} %copy-done.10), channel_id=1, replica_groups=mesh['dp'=16,'tensor'=8] {'dp'}, use_global_device_ids=true, to_apply=%region_10.13 | all-reduce | flops 4096 | bytes 32768 | tf_op jit(solution)/shard_map/psum | solution.py:148
  382.4 1.9 convert_element_type.136
  384.3 7.5 %reduce-scatter.7.cloned.1.call-done = bf16[128,2048]{1,0:T(8,128)(2,1)} async-done(((bf16[2048,2048]{1,0:T(8,128)(2,1)}), bf16[128,2048]{1,0:T(8,128)(2,1)}) %reduce-scatter.7.cloned.1.call-update) | async-done | bytes 524304
  391.8 1.3 copy.82
  (97 shorter events, 20.8 us)
Async XLA Ops:
  7.2 1.1 copy-start
  7.2 9.0 %copy-start.2 = (bf16[192,2048]{1,0:T(8,128)(2,1)S(1)}, bf16[192,2048]{1,0:T(8,128)(2,1)}, u32[]{:S(2)}) copy-start(bf16[192,2048]{1,0:T(8,128)(2,1)} %param.18) | copy-start | bytes 2359300
  7.2 52.4 %all-gather.4.cloned.1.call-start = ((), (), s32[]{:S(2)}) async-start(), calls=%async_computation.4 | async-start | bytes 7077888 | tf_op jit(solution)/shard_map/all_gather | solution.py:87
  16.1 3.2 copy-start.6
  16.1 3.2 copy-start.8
  16.1 3.2 copy-start.20
  16.1 86.8 %all-gather.8.cloned.1.call-start = ((), (), s32[]{:S(2)}) async-start(), calls=%async_computation.6 | async-start | bytes 7077888 | tf_op jit(solution)/shard_map/all_gather | solution.py:110
  18.5 143.1 %all-gather.6.cloned.1.call-start = ((), (), s32[]{:S(2)}) async-start(), calls=%async_computation.5 | async-start | bytes 5570560 | tf_op jit(solution)/shard_map/all_gather | solution.py:93
  19.2 363.2 %reduce-scatter.5.cloned.1.call-start = ((), (), s32[]{:S(2)}) async-start(), calls=%async_computation.7 | async-start | bytes 5570560 | tf_op jit(solution)/shard_map/reduce_scatter | solution.py:132
  20.0 45.9 %copy-start.12 = (pred[8,10]{1,0:T(8,128)(4,1)}, pred[8,10]{1,0:T(8,128)(4,1)S(1)}, u32[]{:S(2)}) copy-start(pred[8,10]{1,0:T(8,128)(4,1)S(1)} %get-tuple-element.57) | copy-start | bytes 244
  20.0 103.6 %copy-start.4 = (s32[8,10]{1,0:T(8,128)}, s32[8,10]{1,0:T(8,128)S(1)}, u32[]{:S(2)}) copy-start(s32[8,10]{1,0:T(8,128)S(1)} %get-tuple-element.53) | copy-start | bytes 964
  20.0 104.3 %copy-start.5 = (s32[8,10]{1,0:T(8,128)}, s32[8,10]{1,0:T(8,128)S(1)}, u32[]{:S(2)}) copy-start(s32[8,10]{1,0:T(8,128)S(1)} %get-tuple-element.56) | copy-start | bytes 964
  21.1 96.6 %copy-start.21 = (pred[10]{0:T(512)(128)(4,1)}, pred[10]{0:T(512)(128)(4,1)S(1)}, u32[]{:S(2)}) copy-start(pred[10]{0:T(512)(128)(4,1)S(1)} %get-tuple-element.44) | copy-start | bytes 34
  127.1 2.0 copy-start.17
  127.1 2.0 copy-start.18
  127.1 0.6 copy-start.15
  127.2 1.9 copy-start.16
  188.1 43.1 %all-to-all-start = ((bf16[192,8,1024]{2,0,1:T(8,128)(2,1)}), bf16[192,8,1024]{2,0,1:T(8,128)(2,1)}, u32[]{:S(2)}, u32[]{:S(2)}) async-start(bf16[192,8,1024]{2,0,1:T(8,128)(2,1)} %copy.63), calls=%async_computation | async-start | bytes 6291456 | tf_op jit(solution)/shard_map/all_to_all | solution.py:100
  207.4 4.2 %copy-start.19 = (bf16[16]{0:T(256)(128)(2,1)S(1)}, bf16[16]{0:T(256)(128)(2,1)}, u32[]{:S(2)}) copy-start(bf16[16]{0:T(256)(128)(2,1)} %reshape.263) | copy-start | bytes 100
  207.4 4.2 %copy-start.22 = (pred[16]{0:T(512)(128)(4,1)S(1)}, pred[16]{0:T(512)(128)(4,1)}, u32[]{:S(2)}) copy-start(pred[16]{0:T(512)(128)(4,1)} %compare_and_fusion.2) | copy-start | bytes 52
  228.3 7.5 %copy-start.7 = (s32[8,10]{1,0:T(8,128)S(1)}, s32[8,10]{1,0:T(8,128)}, u32[]{:S(2)}) copy-start(s32[8,10]{1,0:T(8,128)} %param.20) | copy-start | bytes 964
  228.3 7.5 %copy-start.13 = (pred[8,10]{1,0:T(8,128)(4,1)S(1)}, pred[8,10]{1,0:T(8,128)(4,1)}, u32[]{:S(2)}) copy-start(pred[8,10]{1,0:T(8,128)(4,1)} %get-tuple-element.52) | copy-start | bytes 244
  228.3 7.6 %copy-start.14 = (pred[8,10]{1,0:T(8,128)(4,1)S(1)}, pred[8,10]{1,0:T(8,128)(4,1)}, u32[]{:S(2)}) copy-start(pred[8,10]{1,0:T(8,128)(4,1)} %get-tuple-element.55) | copy-start | bytes 244
  228.3 7.8 %copy-start.9 = (s32[8,10]{1,0:T(8,128)S(1)}, s32[8,10]{1,0:T(8,128)}, u32[]{:S(2)}) copy-start(s32[8,10]{1,0:T(8,128)} %param.19) | copy-start | bytes 964
  231.2 42.9 %all-to-all-start.1 = ((bf16[192,8,1024]{2,0,1:T(8,128)(2,1)}), bf16[192,8,1024]{2,0,1:T(8,128)(2,1)}, u32[]{:S(2)}, u32[]{:S(2)}) async-start(bf16[192,8,1024]{2,0,1:T(8,128)(2,1)} %copy.73), calls=%async_computation.1 | async-start | bytes 6291456 | tf_op jit(solution)/shard_map/all_to_all | solution.py:121
  235.6 156.2 %reduce-scatter.7.cloned.1.call-start = ((), (), s32[]{:S(2)}) async-start(), calls=%async_computation.8 | async-start | bytes 8912896
  287.4 1.1 copy-start.1
  287.4 1.6 copy-start.3
  287.5 1.6 copy-start.11
  308.8 0.7 copy-start.10
Sparse Core Ops, SparseCore 0:
  16.3 43.3 all-gather.3
  61.9 40.9 all-gather.7
  105.0 56.5 all-gather.5
  164.9 78.7 reduce-scatter.4
  309.0 82.7 reduce-scatter.6
where the time goes:
time: 403 us; the launch traced here: 401 us
  waiting for transfers between devices  133 us (33%)
  local copies, waits for them, and re-layouts  113 us (28%)
  blocking collectives  72.9 us (18%)
  matrix products  35.7 us (9%)
  other arithmetic  23.6 us (6%)
  between operations  14.1 us (3%)
  starting transfers between devices  9.25 us (2%)
    psum x1, blocking collectives, on_device(): lax.psum((jnp.sum(grad_pre, axis=0), jnp.sum(grad_mixed, axis=0)), 'dp')  72.9 us
    all_gather x1, waiting for transfers between devices, on_device(): whole_start = lax.all_gather(start, 'tensor', axis=1, tiled=True)  38.5 us
    all_gather x1, waiting for transfers between devices, on_device(): whole_grad = lax.all_gather(grad_mixed_low, 'tensor', axis=1, tiled=True)  37 us
    all_to_all x1, waiting for transfers between devices, on_device(): lax.all_to_all(pack_parts(back_parts, chosen_in, filled_in), 'tensor', sp...  23.4 us
    all_gather x1, waiting for transfers between devices, on_device(): lax.all_gather(cross_blocks, 'dp', axis=1, tiled=True)  22.7 us
    reshape x4, local copies, waits for them, and re-layouts, pack_parts(): picked.reshape(parts.shape[0], chosen.shape[0], chosen.shape[1] * parts.s...  22.1 us
    unnamed x51, local copies, waits for them, and re-layouts  19.4 us
    reshape x2, local copies, waits for them, and re-layouts, collect_parts(): flattened = received.reshape(row_count, groups * capacity, block_width)  11.3 us
  transfers between devices with their start and end apart: 7, of which 6 were waited for; matrix products, arithmetic and copies ran while one was open for 39% of the time, Pallas kernels for 0%

commit v1 on v0

--- a/solution.py
+++ b/solution.py
@@ -90,7 +90,9 @@
     product = jnp.einsum(
         "rki,kij->rkj",
         taken,
-        lax.all_gather(cross_blocks, "dp", axis=1, tiled=True),
+        jnp.concatenate(
+            lax.all_to_all(jnp.stack([cross_blocks] * lax.axis_size("dp")), "dp", 0, 0), axis=1
+        ),
         preferred_element_type=jnp.float32,
     )
     parts = product.astype(jnp.bfloat16) * switch

time: 403 us -> 382 us (0.948)
  waiting for transfers between devices: 133 us -> 97.5 us
  starting transfers between devices: 9.25 us -> 18.1 us
  local copies, waits for them, and re-layouts: 113 us -> 119 us
    all_gather x1, waiting for transfers between devices: 22.7 us -> 0.01 us  [on_device(): lax.all_gather(cross_blocks, 'dp', axis=1, tiled=True)]
    all_gather x1, waiting for transfers between devices: 38.5 us -> 26.9 us  [on_device(): whole_start = lax.all_gather(start, 'tensor', axis=1, tiled=True)]
    all_to_all x0 -> x1, starting transfers between devices: none -> 8.31 us  [on_device(): lax.all_to_all(jnp.stack([cross_blocks] * lax.axis_size('dp')), 'dp', 0, 0)]
    unnamed x51 -> x59, local copies, waits for them, and re-layouts: 19.4 us -> 19.3 us
  transfers between devices with their start and end apart: 7 -> 8, of which waited for: 6 -> 5; matrix products, arithmetic and copies ran while one was open for 39% -> 42% of each run, Pallas kernels for 0% -> 0%
where the time goes in v1:
time: 382 us; the launch traced here: 379 us
  local copies, waits for them, and re-layouts  119 us (31%)
  waiting for transfers between devices  97.5 us (26%)
  blocking collectives  75.2 us (20%)
  matrix products  32.6 us (9%)
  other arithmetic  23.3 us (6%)
  starting transfers between devices  18.1 us (5%)
  between operations  14.1 us (4%)
    psum x1, blocking collectives, on_device(): lax.psum((jnp.sum(grad_pre, axis=0), jnp.sum(grad_mixed, axis=0)), 'dp')  75.2 us
    all_gather x1, waiting for transfers between devices, on_device(): whole_grad = lax.all_gather(grad_mixed_low, 'tensor', axis=1, tiled=True)  37 us
    all_gather x1, waiting for transfers between devices, on_device(): whole_start = lax.all_gather(start, 'tensor', axis=1, tiled=True)  26.9 us
    all_to_all x1, waiting for transfers between devices, on_device(): lax.all_to_all(pack_parts(back_parts, chosen_in, filled_in), 'tensor', sp...  23.1 us
    reshape x4, local copies, waits for them, and re-layouts, pack_parts(): picked.reshape(parts.shape[0], chosen.shape[0], chosen.shape[1] * parts.s...  22.1 us
    unnamed x59, local copies, waits for them, and re-layouts  19.3 us
    reshape x2, local copies, waits for them, and re-layouts, collect_parts(): flattened = received.reshape(row_count, groups * capacity, block_width)  11.3 us
    all_to_all x1, starting transfers between devices, on_device(): lax.all_to_all(jnp.stack([cross_blocks] * lax.axis_size('dp')), 'dp', 0, 0)  8.31 us
  transfers between devices with their start and end apart: 8, of which 5 were waited for; matrix products, arithmetic and copies ran while one was open for 42% of the time, Pallas kernels for 0%

profile of v1, /device:TPU:0, one launch (start us, length us, event | category | flops | bytes accessed | tf_op | source)
XLA Modules:
  0.0 379.5 jit_solution(15094301369606145670)
XLA Ops:
  8.3 7.8 %fusion.9 = (f32[2048]{0:T(1024)}, bf16[192,2048]{1,0:T(8,128)(2,1)}, f32[192,2048]{1,0:T(8,128)}) fusion(bf16[192,2048]{1,0:T(8,128)(2,1)} %param.18, f32[2048]{0:T(1024)} %param.15, bf16[192,2048]{1,0:T(8,128)(2,1)S(1)} %copy-done, bf16[2048,2048]{1,0:T(8,128)(2,1)} %param.14), kind=kOutput, calls=%fused_computation.28 | convolution fusion | flops 1614542848 | bytes 12337152 | tf_op jit(solution)/shard_map/dot_general | solution.py:72
  16.2 2.3 fusion.10
  19.3 3.1 stack.2
  22.3 8.3 %all-to-all-start = ((bf16[16,10,32,512]{3,2,1,0:T(8,128)(2,1)}), bf16[16,10,32,512]{3,2,1,0:T(8,128)(2,1)}, u32[]{:S(2)}, u32[]{:S(2)}) async-start(bf16[16,10,32,512]{3,2,1,0:T(8,128)(2,1)} %stack.2), calls=%async_computation | async-start | bytes 10485760 | tf_op jit(solution)/shard_map/all_to_all | solution.py:94
  32.7 26.9 %all-gather.4.cloned.1.call-done = bf16[192,16384]{1,0:T(8,128)(2,1)} async-done(((bf16[192,2048]{1,0:T(8,128)(2,1)}), bf16[192,16384]{1,0:T(8,128)(2,1)}) %all-gather.4.cloned.1.call-update) | async-done | bytes 6291472 | tf_op jit(solution)/shard_map/all_gather | solution.py:87
  59.6 6.2 %copy.93 = bf16[24,32,8,512]{3,2,0,1:T(8,128)(2,1)} copy(bf16[24,32,8,512]{3,2,1,0:T(8,128)(2,1)} %bitcast.73) | data formatting | bytes 12582912 | tf_op jit(solution)/shard_map/reshape | solution.py:88
  65.8 37.0 %all-gather.6.cloned.1.call-done = bf16[192,16384]{1,0:T(8,128)(2,1)} async-done(((bf16[192,2048]{1,0:T(8,128)(2,1)}), bf16[192,16384]{1,0:T(8,128)(2,1)}) %all-gather.6.cloned.1.call-update) | async-done | bytes 6291472 | tf_op jit(solution)/shard_map/all_gather | solution.py:112
  102.9 6.3 %copy.92 = bf16[24,32,8,512]{3,2,0,1:T(8,128)(2,1)} copy(bf16[24,32,8,512]{3,2,1,0:T(8,128)(2,1)} %bitcast.74) | data formatting | bytes 12582912 | tf_op jit(solution)/shard_map/reshape | solution.py:113
  109.1 4.9 %gather_fusion = bf16[10,192,512]{2,1,0:T(8,128)(2,1)} fusion(bf16[192,32,512]{2,0,1:T(8,128)(2,1)} %bitcast.71, s32[1024]{0:T(1024)S(1)} %pad_clamp_fusion.3), kind=kCustom, calls=%fused_computation.clone | custom fusion | bytes 3932200 | tf_op jit(solution)/shard_map/jit(_take)/gather | solution.py:88
  114.0 3.7 gather_fusion.2
  117.7 5.8 %convolution_convert_fusion = bf16[10,512,512]{2,1,0:T(8,128)(2,1)} fusion(bf16[10,192,512]{2,1,0:T(8,128)(2,1)} %gather_fusion, pred[10]{0:T(512)(128)(4,1)} %get-tuple-element.48, bf16[10,192,512]{2,1,0:T(8,128)(2,1)S(1)} %gather_fusion.2, pred[10]{0:T(512)(128)(4,1)S(1)} %get-tuple-element.44, bf16[10]{0:T(256)(128)(2,1)} %get-tuple-element.50), kind=kOutput, calls=%fused_computation.9 | convolution fusion | flops 1012203520 | bytes 9175080 | tf_op jit(solution)/shard_map/rki,rkj->kij/dot_general | solution.py:133
  127.7 1.3 select_reduce_fusion
  129.0 1.3 copy.61
  130.3 1.3 reshape.263
  131.6 1.3 fusion.14
  133.5 1.3 copy.64
  138.4 3.1 copy.63
  141.5 2.6 multiply_bitcast_fusion
  144.1 4.1 %gather_fusion.1 = bf16[16,192,512]{2,1,0:T(8,128)(2,1)} fusion(bf16[192,10,512]{2,0,1:T(8,128)(2,1)} %multiply_bitcast_fusion, s32[1024]{0:T(1024)} %pad_clamp_fusion.2), kind=kCustom, calls=%fused_computation.1.clone | custom fusion | bytes 6291520 | tf_op jit(solution)/shard_map/jit(_take)/gather | solution.py:30
  148.2 2.3 bitcast_multiply_fusion.1
  150.5 3.4 copy.65
  154.0 5.7 %reshape.264 = bf16[192,8,1024]{2,1,0:T(8,128)(2,1)} reshape(bf16[192,16,512]{2,1,0:T(8,128)(2,1)} %copy.65) | data formatting | bytes 6291456 | tf_op jit(solution)/shard_map/reshape | solution.py:33
  159.7 5.3 %copy.66 = bf16[192,8,1024]{2,0,1:T(8,128)(2,1)} copy(bf16[192,8,1024]{2,1,0:T(8,128)(2,1)} %reshape.264) | data formatting | bytes 6291456 | tf_op jit(solution)/shard_map/reshape | solution.py:33
  165.0 4.7 %all-to-all-start.1 = ((bf16[192,8,1024]{2,0,1:T(8,128)(2,1)}), bf16[192,8,1024]{2,0,1:T(8,128)(2,1)}, u32[]{:S(2)}, u32[]{:S(2)}) async-start(bf16[192,8,1024]{2,0,1:T(8,128)(2,1)} %copy.66), calls=%async_computation.1 | async-start | bytes 6291456 | tf_op jit(solution)/shard_map/all_to_all | solution.py:102
  169.6 1.3 copy.72
  174.7 1.3 reshape.273
  178.4 5.8 %convert_bitcast_fusion.1 = bf16[192,10,512]{2,0,1:T(8,128)(2,1)} fusion(bf16[10,512,512]{2,1,0:T(8,128)(2,1)} %all-gather.8.cloned.1.call-done, bf16[10,192,512]{2,1,0:T(8,128)(2,1)S(1)} %gather_fusion.2, pred[10]{0:T(512)(128)(4,1)} %copy-done.23, bf16[10]{0:T(256)(128)(2,1)} %get-tuple-element.50), kind=kOutput, calls=%fused_computation.19 | convolution fusion | flops 1009582080 | bytes 9175070 | tf_op jit(solution)/shard_map/rkj,kij->rki/dot_general | solution.py:115
  184.2 4.2 %gather_fusion.3 = bf16[16,192,512]{2,1,0:T(8,128)(2,1)} fusion(bf16[192,10,512]{2,0,1:T(8,128)(2,1)} %convert_bitcast_fusion.1, s32[1024]{0:T(1024)} %pad_clamp_fusion), kind=kCustom, calls=%fused_computation.3.clone | custom fusion | bytes 6291520 | tf_op jit(solution)/shard_map/jit(_take)/gather | solution.py:30
  188.4 2.3 bitcast_multiply_fusion
  190.6 3.5 copy.75
  194.1 5.7 %reshape.269 = bf16[192,8,1024]{2,1,0:T(8,128)(2,1)} reshape(bf16[192,16,512]{2,1,0:T(8,128)(2,1)} %copy.75) | data formatting | bytes 6291456 | tf_op jit(solution)/shard_map/reshape | solution.py:33
  199.8 5.4 %copy.76 = bf16[192,8,1024]{2,0,1:T(8,128)(2,1)} copy(bf16[192,8,1024]{2,1,0:T(8,128)(2,1)} %reshape.269) | data formatting | bytes 6291456 | tf_op jit(solution)/shard_map/reshape | solution.py:33
  205.2 2.7 all-to-all-done.1
  207.9 4.5 %all-to-all-start.2 = ((bf16[192,8,1024]{2,0,1:T(8,128)(2,1)}), bf16[192,8,1024]{2,0,1:T(8,128)(2,1)}, u32[]{:S(2)}, u32[]{:S(2)}) async-start(bf16[192,8,1024]{2,0,1:T(8,128)(2,1)} %copy.76), calls=%async_computation.2 | async-start | bytes 6291456 | tf_op jit(solution)/shard_map/all_to_all | solution.py:123
  213.6 5.3 %copy.67 = bf16[192,8,1024]{2,1,0:T(8,128)(2,1)} copy(bf16[192,8,1024]{2,0,1:T(8,128)(2,1)} %all-to-all-done.1) | data formatting | bytes 6291456 | tf_op jit(solution)/shard_map/all_to_all | solution.py:102
  218.9 5.7 %reshape.265 = bf16[192,16,512]{2,1,0:T(8,128)(2,1)} reshape(bf16[192,8,1024]{2,1,0:T(8,128)(2,1)} %copy.67) | data formatting | bytes 6291456 | tf_op jit(solution)/shard_map/reshape | solution.py:50
  224.6 2.5 fusion.29
  227.7 23.1 %all-to-all-done.2 = bf16[192,8,1024]{2,0,1:T(8,128)(2,1)} async-done(((bf16[192,8,1024]{2,0,1:T(8,128)(2,1)}), bf16[192,8,1024]{2,0,1:T(8,128)(2,1)}, u32[]{:S(2)}, u32[]{:S(2)}) %all-to-all-start.2) | async-done | bytes 3145760 | tf_op jit(solution)/shard_map/all_to_all | solution.py:123
  250.8 5.3 %copy.77 = bf16[192,8,1024]{2,1,0:T(8,128)(2,1)} copy(bf16[192,8,1024]{2,0,1:T(8,128)(2,1)} %all-to-all-done.2) | data formatting | bytes 6291456 | tf_op jit(solution)/shard_map/all_to_all | solution.py:123
  256.0 5.7 %reshape.270 = bf16[192,16,512]{2,1,0:T(8,128)(2,1)} reshape(bf16[192,8,1024]{2,1,0:T(8,128)(2,1)} %copy.77) | data formatting | bytes 6291456 | tf_op jit(solution)/shard_map/reshape | solution.py:50
  261.7 2.5 fusion.30
  265.9 1.9 fusion.26
  267.7 5.6 %convert_bitcast_fusion = bf16[2048,2048]{0,1:T(8,128)(2,1)} fusion(bf16[192,2048]{1,0:T(8,128)(2,1)S(1)} %copy-done, bf16[192,2048]{1,0:T(8,128)(2,1)S(1)} %get-tuple-element.43), kind=kOutput, calls=%fused_computation.4 | convolution fusion | flops 1614807040 | bytes 9961472 | tf_op jit(solution)/shard_map/dot_general | solution.py:143
  273.4 12.2 %copy.84 = bf16[2048,2048]{1,0:T(8,128)(2,1)} copy(bf16[2048,2048]{0,1:T(8,128)(2,1)} %convert_bitcast_fusion) | data formatting | bytes 16777216
  286.2 75.2 %all-reduce = (f32[2048]{0:T(1024)}, f32[2048]{0:T(1024)}) all-reduce(f32[2048]{0:T(1024)S(1)} %get-tuple-element.42, f32[2048]{0:T(1024)S(1)} %copy-done.12), channel_id=1, replica_groups=mesh['dp'=16,'tensor'=8] {'dp'}, use_global_device_ids=true, to_apply=%region_10.13 | all-reduce | flops 4096 | bytes 32768 | tf_op jit(solution)/shard_map/psum | solution.py:150
  361.4 1.9 convert_element_type.136
  363.3 7.1 %reduce-scatter.7.cloned.1.call-done = bf16[128,2048]{1,0:T(8,128)(2,1)} async-done(((bf16[2048,2048]{1,0:T(8,128)(2,1)}), bf16[128,2048]{1,0:T(8,128)(2,1)}) %reduce-scatter.7.cloned.1.call-update) | async-done | bytes 524304
  370.4 1.3 copy.85
  (110 shorter events, 23.6 us)
Async XLA Ops:
  7.2 1.1 copy-start
  7.2 9.0 %copy-start.3 = (bf16[192,2048]{1,0:T(8,128)(2,1)S(1)}, bf16[192,2048]{1,0:T(8,128)(2,1)}, u32[]{:S(2)}) copy-start(bf16[192,2048]{1,0:T(8,128)(2,1)} %param.18) | copy-start | bytes 2359300
  7.2 52.4 %all-gather.4.cloned.1.call-start = ((), (), s32[]{:S(2)}) async-start(), calls=%async_computation.5 | async-start | bytes 7077888 | tf_op jit(solution)/shard_map/all_gather | solution.py:87
  16.1 3.2 copy-start.5
  16.1 86.8 %all-gather.6.cloned.1.call-start = ((), (), s32[]{:S(2)}) async-start(), calls=%async_computation.6 | async-start | bytes 7077888 | tf_op jit(solution)/shard_map/all_gather | solution.py:112
  18.5 159.9 %all-gather.8.cloned.1.call-start = ((), (), s32[]{:S(2)}) async-start(), calls=%async_computation.7 | async-start | bytes 5570560 | tf_op jit(solution)/shard_map/all_gather | solution.py:118
  22.3 8.6 %copy-start.10 = (s32[8,10]{1,0:T(8,128)S(1)}, s32[8,10]{1,0:T(8,128)}, u32[]{:S(2)}) copy-start(s32[8,10]{1,0:T(8,128)} %param.19) | copy-start | bytes 964
  22.3 9.1 %copy-start.8 = (s32[8,10]{1,0:T(8,128)S(1)}, s32[8,10]{1,0:T(8,128)}, u32[]{:S(2)}) copy-start(s32[8,10]{1,0:T(8,128)} %param.20) | copy-start | bytes 964
  22.3 9.1 %copy-start.22 = (s32[8]{0:T(128)S(1)}, s32[8]{0:T(128)}, u32[]{:S(2)}) copy-start(s32[8]{0:T(128)} %param.21) | copy-start | bytes 100
  22.3 116.1 %all-to-all-start = ((bf16[16,10,32,512]{3,2,1,0:T(8,128)(2,1)}), bf16[16,10,32,512]{3,2,1,0:T(8,128)(2,1)}, u32[]{:S(2)}, u32[]{:S(2)}) async-start(bf16[16,10,32,512]{3,2,1,0:T(8,128)(2,1)} %stack.2), calls=%async_computation | async-start | bytes 10485760 | tf_op jit(solution)/shard_map/all_to_all | solution.py:94
  30.7 330.8 %reduce-scatter.5.cloned.1.call-start = ((), (), s32[]{:S(2)}) async-start(), calls=%async_computation.8 | async-start | bytes 5570560 | tf_op jit(solution)/shard_map/reduce_scatter | solution.py:134
  31.5 86.3 %copy-start.23 = (pred[10]{0:T(512)(128)(4,1)}, pred[10]{0:T(512)(128)(4,1)S(1)}, u32[]{:S(2)}) copy-start(pred[10]{0:T(512)(128)(4,1)S(1)} %get-tuple-element.44) | copy-start | bytes 34
  32.1 33.8 %copy-start.14 = (pred[8,10]{1,0:T(8,128)(4,1)}, pred[8,10]{1,0:T(8,128)(4,1)S(1)}, u32[]{:S(2)}) copy-start(pred[8,10]{1,0:T(8,128)(4,1)S(1)} %get-tuple-element.57) | copy-start | bytes 244
  32.1 91.5 %copy-start.6 = (s32[8,10]{1,0:T(8,128)}, s32[8,10]{1,0:T(8,128)S(1)}, u32[]{:S(2)}) copy-start(s32[8,10]{1,0:T(8,128)S(1)} %get-tuple-element.53) | copy-start | bytes 964
  32.1 92.2 %copy-start.7 = (s32[8,10]{1,0:T(8,128)}, s32[8,10]{1,0:T(8,128)S(1)}, u32[]{:S(2)}) copy-start(s32[8,10]{1,0:T(8,128)S(1)} %get-tuple-element.56) | copy-start | bytes 964
  127.1 1.9 copy-start.19
  127.1 1.9 copy-start.20
  127.1 0.5 copy-start.17
  127.2 1.8 copy-start.18
  138.4 3.1 copy-start.2
  138.4 3.1 copy-start.24
  138.4 3.1 copy-start.25
  165.0 42.9 %all-to-all-start.1 = ((bf16[192,8,1024]{2,0,1:T(8,128)(2,1)}), bf16[192,8,1024]{2,0,1:T(8,128)(2,1)}, u32[]{:S(2)}, u32[]{:S(2)}) async-start(bf16[192,8,1024]{2,0,1:T(8,128)(2,1)} %copy.66), calls=%async_computation.1 | async-start | bytes 6291456 | tf_op jit(solution)/shard_map/all_to_all | solution.py:102
  184.2 4.2 %copy-start.21 = (bf16[16]{0:T(256)(128)(2,1)S(1)}, bf16[16]{0:T(256)(128)(2,1)}, u32[]{:S(2)}) copy-start(bf16[16]{0:T(256)(128)(2,1)} %reshape.273) | copy-start | bytes 100
  184.2 4.2 %copy-start.26 = (pred[16]{0:T(512)(128)(4,1)S(1)}, pred[16]{0:T(512)(128)(4,1)}, u32[]{:S(2)}) copy-start(pred[16]{0:T(512)(128)(4,1)} %compare_and_fusion.2) | copy-start | bytes 52
  205.2 7.6 %copy-start.9 = (s32[8,10]{1,0:T(8,128)S(1)}, s32[8,10]{1,0:T(8,128)}, u32[]{:S(2)}) copy-start(s32[8,10]{1,0:T(8,128)} %param.20) | copy-start | bytes 964
  205.2 7.6 %copy-start.15 = (pred[8,10]{1,0:T(8,128)(4,1)S(1)}, pred[8,10]{1,0:T(8,128)(4,1)}, u32[]{:S(2)}) copy-start(pred[8,10]{1,0:T(8,128)(4,1)} %get-tuple-element.52) | copy-start | bytes 244
  205.2 7.7 %copy-start.16 = (pred[8,10]{1,0:T(8,128)(4,1)S(1)}, pred[8,10]{1,0:T(8,128)(4,1)}, u32[]{:S(2)}) copy-start(pred[8,10]{1,0:T(8,128)(4,1)} %get-tuple-element.55) | copy-start | bytes 244
  205.2 8.0 %copy-start.11 = (s32[8,10]{1,0:T(8,128)S(1)}, s32[8,10]{1,0:T(8,128)}, u32[]{:S(2)}) copy-start(s32[8,10]{1,0:T(8,128)} %param.19) | copy-start | bytes 964
  207.9 42.9 %all-to-all-start.2 = ((bf16[192,8,1024]{2,0,1:T(8,128)(2,1)}), bf16[192,8,1024]{2,0,1:T(8,128)(2,1)}, u32[]{:S(2)}, u32[]{:S(2)}) async-start(bf16[192,8,1024]{2,0,1:T(8,128)(2,1)} %copy.76), calls=%async_computation.2 | async-start | bytes 6291456 | tf_op jit(solution)/shard_map/all_to_all | solution.py:123
  212.3 158.1 %reduce-scatter.7.cloned.1.call-start = ((), (), s32[]{:S(2)}) async-start(), calls=%async_computation.9 | async-start | bytes 8912896
  264.2 1.1 copy-start.1
  264.2 1.6 copy-start.4
  264.2 1.6 copy-start.13
  285.6 0.7 copy-start.12
Sparse Core Ops, SparseCore 0:
  16.2 43.3 all-gather.3
  61.9 40.9 all-gather.5
  105.0 56.5 all-gather.7
  164.9 78.6 reduce-scatter.4
  285.7 84.6 reduce-scatter.6
